TPU v7x, 32 devices: a whole 2x2x4 slice. The times are simulated.
32 devices in a mesh: groups: 2 (over x), row: 8 (over z, y), col: 2 (over core).
Axes of the slice: x: 2, y: 2, z: 4, core: 2. Of those that a mesh axis runs over, the one named last changes fastest.
Arguments:
- spectra: bfloat16 [4096, 16384], P(('groups', 'row', 'col')), parts along dimension 0, may hold values from -60 to 60
- block_order: int32 [4096], P('groups'), parts along dimension 0, may hold values from 0 to 2047, each once
- offsets: int32 [17], replicated, may hold values from -24 to 24, as said below
Outputs:
- similarity: float32 [4096, 2048], P(('groups', 'row', 'col')), parts along dimension 0
There are 2 independent parts, one for each index of `groups`. A program takes and returns all parts, laid end to end along the dimension named above; an argument that names none is the same for every part. Nothing has to cross between parts.
Inputs may be any that keep to these rules, and one draw needn't show every extreme that they name: `offsets`: the 17 values are distinct, include 0 and 24, and the negative of each value is also among them.
All inputs are finite; a program needn't handle non-finite values.
Results may differ from a plain program's by a relative error of at most 0.0013.
Values may be sent and summed in bfloat16 or wider, within the bound.
A program may use at most 128 MiB of HBM per device.

v0:
```python
import math

import jax
import jax.numpy as jnp
from jax import lax
from jax.sharding import PartitionSpec as P

TAPS = 16
PADW = 64


def taps_table(count):
    steps = jnp.arange(count, dtype=jnp.float32)
    return (0.5 - 0.5 * jnp.cos(2.0 * math.pi * (steps + 0.5) / count)).astype(jnp.bfloat16)


def shifted_stack(mine, offsets):
    coarse_len = mine.shape[1]
    mine_padded = jnp.pad(mine, ((0, 0), (PADW, PADW)))

    def moved(offset):
        return lax.dynamic_slice_in_dim(mine_padded, PADW - offset, coarse_len, 1)

    stacked = jax.vmap(moved)(offsets)
    return stacked.reshape(-1, coarse_len)


def strip_scores(stacked, extended, first_block, block_rows, width_blocks):
    panel = lax.dynamic_slice_in_dim(
        extended, first_block * block_rows, width_blocks * block_rows, 0
    )
    scores = lax.dot_general(
        stacked, panel, (((1,), (1,)), ((), ())), preferred_element_type=jnp.float32
    )
    scores = scores.reshape(-1, block_rows, width_blocks, block_rows)
    return jnp.max(scores, axis=0)


def per_device(spectra, block_order, offsets):
    block_rows, bins = spectra.shape
    coarse_len = bins // TAPS
    group = min(128, coarse_len)
    weights = jnp.kron(
        jnp.eye(group, dtype=jnp.float32), taps_table(TAPS).astype(jnp.float32)[:, None]
    ).astype(jnp.bfloat16)
    windows = spectra.reshape(block_rows * coarse_len // group, TAPS * group)
    coarse = jnp.dot(windows, weights, preferred_element_type=jnp.float32).reshape(
        block_rows, coarse_len
    )
    scale = lax.rsqrt(jnp.mean(coarse * coarse, axis=1, keepdims=True) + 1e-06) * (
        1.0 / math.sqrt(coarse_len)
    )
    unit = (coarse * scale).astype(jnp.bfloat16)
    every = lax.all_gather(unit, ("row", "col"), axis=0, tiled=True)
    ordered = jnp.take(every, block_order, axis=0)
    total_rows = ordered.shape[0]
    blocks = lax.axis_size("row") * lax.axis_size("col")
    myself = lax.axis_index("row") * lax.axis_size("col") + lax.axis_index("col")
    mine = lax.dynamic_slice_in_dim(ordered, myself * block_rows, block_rows, 0)
    stacked = shifted_stack(mine, offsets)
    extended = jnp.concatenate([ordered, ordered[:block_rows]], axis=0)
    empty = jnp.zeros((blocks, block_rows, block_rows), jnp.float32)

    def place(acc, first):
        scores = strip_scores(stacked, extended, first, block_rows, 2)
        acc = lax.dynamic_update_slice_in_dim(acc, scores[None, :, 0, :], first, 0)
        return lax.dynamic_update_slice_in_dim(acc, scores[None, :, 1, :], (first + 1) % blocks, 0)

    result = lax.fori_loop(0, blocks // 2, lambda pair, acc: place(acc, 2 * pair), empty)
    return jnp.transpose(result, (1, 0, 2)).reshape(block_rows, total_rows)


def solution(mesh):
    in_specs = (P(("groups", "row", "col"), None), P("groups"), P())
    out_specs = P(("groups", "row", "col"), None)
    return jax.shard_map(
        per_device, mesh=mesh, in_specs=in_specs, out_specs=out_specs, check_vma=False
    )
```

profile of v0, /device:TPU:0, one launch (start us, length us, event | category | flops | bytes accessed | tf_op | source)
XLA Modules:
  0.0 212.4 jit_solution(15265125319011555981)
XLA Ops:
  6.6 7.4 %reshape.96 = bf16[1024,2048]{1,0:T(8,128)(2,1)} reshape(bf16[128,16384]{1,0:T(8,128)(2,1)} %param.5) | data formatting | bytes 8388608 | tf_op jit(solution)/shard_map/reshape | solution.py:46
  14.2 3.7 %multiply_reduce_fusion = (f32[1024]{0:T(1024)S(1)}, f32[1024,128]{0,1:T(8,128)S(1)}) fusion(bf16[2048,128]{1,0:T(8,128)(2,1)S(1)} %bitcast.40, bf16[1024,2048]{1,0:T(8,128)(2,1)} %reshape.96), kind=kOutput, calls=%fused_computation.14 | convolution fusion | flops 537132032 | bytes 5246976 | tf_op jit(solution)/shard_map/dot_general | solution.py:47
  19.4 53.3 %all-gather.2.cloned.1.call-done = bf16[2048,1024]{1,0:T(8,128)(2,1)} async-done(((bf16[128,1024]{1,0:T(8,128)(2,1)}), bf16[2048,1024]{1,0:T(8,128)(2,1)}) %all-gather.2.cloned.1.call-update) | async-done | bytes 4194320 | tf_op jit(solution)/shard_map/all_gather | solution.py:54
  72.7 13.7 %gather_fusion = bf16[2048,1024]{1,0:T(8,128)(2,1)} fusion(bf16[2048,1024]{1,0:T(8,128)(2,1)} %all-gather.2.cloned.1.call-done, s32[2048]{0:T(1024)S(1)} %fusion.3), kind=kCustom, calls=%fused_computation | custom fusion | bytes 8396800 | tf_op jit(solution)/shard_map/jit(_take)/gather | solution.py:55
  86.4 2.5 %broadcast_select_fusion = bf16[2048,1024]{1,0:T(8,128)(2,1)S(1)} fusion(bf16[2048,1024]{1,0:T(8,128)(2,1)} %gather_fusion, pred[2048]{0:T(1024)(128)(4,1)S(1)} %compare_and_fusion), kind=kLoop, calls=%fused_computation.9 | loop fusion | flops 2097152 | bytes 8390656 | tf_op jit(solution)/shard_map/jit(_take)/select_n | solution.py:55
  89.0 2.5 %pad_maximum_fusion = bf16[2176,1024]{1,0:T(8,128)(2,1)} fusion(bf16[128,1024]{1,0:T(8,128)(2,1)S(1)} %get-tuple-element.145, bf16[2048,1024]{1,0:T(8,128)(2,1)S(1)} %broadcast_select_fusion), kind=kLoop, calls=%fused_computation.8 | loop fusion | flops 8912896 | bytes 8912896 | tf_op jit(solution)/shard_map/concatenate | solution.py:61
  91.7 35.6 %while.17 = (s32[]{:T(128)}, bf16[128,1152]{1,0:T(8,128)(2,1)S(1)}, s32[17,2]{0,1:T(2,128)S(1)}, bf16[17,128,1024]{2,1,0:T(8,128)(2,1)}, s32[]{:T(128)}) while((s32[]{:T(128)}, bf16[128,1152]{1,0:T(8,128)(2,1)S(1)}, s32[17,2]{0,1:T(2,128)S(1)}, bf16[17,128,1024]{2,1,0:T(8,128)(2,1)}, s32[]{:T(128)}) %tuple.52), condition=%wide.while_cond, body=%wide.while_body.sunk | while | flops 2 | bytes 525401 | solution.py:22
  92.3 1.5 bitcast_dynamic-update-slice_fusion.8
  94.3 1.5 bitcast_dynamic-update-slice_fusion.8
  96.4 1.5 bitcast_dynamic-update-slice_fusion.8
  98.5 1.5 bitcast_dynamic-update-slice_fusion.8
  100.6 1.5 bitcast_dynamic-update-slice_fusion.8
  102.7 1.5 bitcast_dynamic-update-slice_fusion.8
  104.8 1.5 bitcast_dynamic-update-slice_fusion.8
  106.9 1.5 bitcast_dynamic-update-slice_fusion.8
  109.0 1.5 bitcast_dynamic-update-slice_fusion.8
  111.1 1.5 bitcast_dynamic-update-slice_fusion.8
  113.2 1.5 bitcast_dynamic-update-slice_fusion.8
  117.4 1.5 bitcast_dynamic-update-slice_fusion.8
  119.4 1.5 bitcast_dynamic-update-slice_fusion.8
  121.5 1.5 bitcast_dynamic-update-slice_fusion.8
  123.6 1.5 bitcast_dynamic-update-slice_fusion.8
  125.7 1.5 bitcast_dynamic-update-slice_fusion.8
  127.3 77.2 %while.16 = (s32[]{:T(128)}, f32[16,128,128]{2,1,0:T(8,128)S(1)}, bf16[2176,1024]{1,0:T(8,128)(2,1)}, bf16[2176,1024]{1,0:T(8,128)(2,1)}, s32[]{:T(128)}, /*inde...) while((s32[]{:T(128)}, f32[16,128,128]{2,1,0:T(8,128)S(1)}, ...), condition=%wide.region_4.5_spmd, body=%wide.region_2.4_spmd.sunk | while | flops 1141374976 | bytes 19005812 | solution.py:69
  127.4 3.9 %convolution_bitcast_fusion.3 = f32[2176,256]{0,1:T(8,128)S(1)} fusion(bf16[2176,1024]{1,0:T(8,128)(2,1)} %get-tuple-element.244, bf16[2176,1024]{1,0:T(8,128)(2,1)} %get-tuple-element.243, s32[]{:T(128)S(6)} %select_n.83), kind=kOutput, calls=%fused_computation.1.clone.1 | convolution fusion | flops 1140850688 | bytes 7208964 | tf_op jit(solution)/shard_map/while/body/eval_jaxpr/dot_general | solution.py:32
  131.2 2.0 copy.14
  133.2 2.7 %reshape.129 = f32[17,128,2,128]{3,2,1,0:T(2,128)S(1)} reshape(f32[2176,256]{1,0:T(8,128)} %copy.14) | data formatting | bytes 4456448 | tf_op jit(solution)/shard_map/while/body/eval_jaxpr/reshape | solution.py:35
  137.0 3.9 %convolution_bitcast_fusion.3 = f32[2176,256]{0,1:T(8,128)S(1)} fusion(bf16[2176,1024]{1,0:T(8,128)(2,1)} %get-tuple-element.244, bf16[2176,1024]{1,0:T(8,128)(2,1)} %get-tuple-element.243, s32[]{:T(128)S(6)} %select_n.83), kind=kOutput, calls=%fused_computation.1.clone.1 | convolution fusion | flops 1140850688 | bytes 7208964 | tf_op jit(solution)/shard_map/while/body/eval_jaxpr/dot_general | solution.py:32
  140.9 2.0 copy.14
  142.8 2.7 %reshape.129 = f32[17,128,2,128]{3,2,1,0:T(2,128)S(1)} reshape(f32[2176,256]{1,0:T(8,128)} %copy.14) | data formatting | bytes 4456448 | tf_op jit(solution)/shard_map/while/body/eval_jaxpr/reshape | solution.py:35
  146.7 3.9 %convolution_bitcast_fusion.3 = f32[2176,256]{0,1:T(8,128)S(1)} fusion(bf16[2176,1024]{1,0:T(8,128)(2,1)} %get-tuple-element.244, bf16[2176,1024]{1,0:T(8,128)(2,1)} %get-tuple-element.243, s32[]{:T(128)S(6)} %select_n.83), kind=kOutput, calls=%fused_computation.1.clone.1 | convolution fusion | flops 1140850688 | bytes 7208964 | tf_op jit(solution)/shard_map/while/body/eval_jaxpr/dot_general | solution.py:32
  150.5 2.0 copy.14
  152.5 2.7 %reshape.129 = f32[17,128,2,128]{3,2,1,0:T(2,128)S(1)} reshape(f32[2176,256]{1,0:T(8,128)} %copy.14) | data formatting | bytes 4456448 | tf_op jit(solution)/shard_map/while/body/eval_jaxpr/reshape | solution.py:35
  156.3 3.9 %convolution_bitcast_fusion.3 = f32[2176,256]{0,1:T(8,128)S(1)} fusion(bf16[2176,1024]{1,0:T(8,128)(2,1)} %get-tuple-element.244, bf16[2176,1024]{1,0:T(8,128)(2,1)} %get-tuple-element.243, s32[]{:T(128)S(6)} %select_n.83), kind=kOutput, calls=%fused_computation.1.clone.1 | convolution fusion | flops 1140850688 | bytes 7208964 | tf_op jit(solution)/shard_map/while/body/eval_jaxpr/dot_general | solution.py:32
  160.2 2.0 copy.14
  162.1 2.7 %reshape.129 = f32[17,128,2,128]{3,2,1,0:T(2,128)S(1)} reshape(f32[2176,256]{1,0:T(8,128)} %copy.14) | data formatting | bytes 4456448 | tf_op jit(solution)/shard_map/while/body/eval_jaxpr/reshape | solution.py:35
  165.9 3.9 %convolution_bitcast_fusion.3 = f32[2176,256]{0,1:T(8,128)S(1)} fusion(bf16[2176,1024]{1,0:T(8,128)(2,1)} %get-tuple-element.244, bf16[2176,1024]{1,0:T(8,128)(2,1)} %get-tuple-element.243, s32[]{:T(128)S(6)} %select_n.83), kind=kOutput, calls=%fused_computation.1.clone.1 | convolution fusion | flops 1140850688 | bytes 7208964 | tf_op jit(solution)/shard_map/while/body/eval_jaxpr/dot_general | solution.py:32
  169.8 2.0 copy.14
  171.8 2.7 %reshape.129 = f32[17,128,2,128]{3,2,1,0:T(2,128)S(1)} reshape(f32[2176,256]{1,0:T(8,128)} %copy.14) | data formatting | bytes 4456448 | tf_op jit(solution)/shard_map/while/body/eval_jaxpr/reshape | solution.py:35
  175.6 3.9 %convolution_bitcast_fusion.3 = f32[2176,256]{0,1:T(8,128)S(1)} fusion(bf16[2176,1024]{1,0:T(8,128)(2,1)} %get-tuple-element.244, bf16[2176,1024]{1,0:T(8,128)(2,1)} %get-tuple-element.243, s32[]{:T(128)S(6)} %select_n.83), kind=kOutput, calls=%fused_computation.1.clone.1 | convolution fusion | flops 1140850688 | bytes 7208964 | tf_op jit(solution)/shard_map/while/body/eval_jaxpr/dot_general | solution.py:32
  179.5 2.0 copy.14
  181.4 2.7 %reshape.129 = f32[17,128,2,128]{3,2,1,0:T(2,128)S(1)} reshape(f32[2176,256]{1,0:T(8,128)} %copy.14) | data formatting | bytes 4456448 | tf_op jit(solution)/shard_map/while/body/eval_jaxpr/reshape | solution.py:35
  185.2 3.9 %convolution_bitcast_fusion.3 = f32[2176,256]{0,1:T(8,128)S(1)} fusion(bf16[2176,1024]{1,0:T(8,128)(2,1)} %get-tuple-element.244, bf16[2176,1024]{1,0:T(8,128)(2,1)} %get-tuple-element.243, s32[]{:T(128)S(6)} %select_n.83), kind=kOutput, calls=%fused_computation.1.clone.1 | convolution fusion | flops 1140850688 | bytes 7208964 | tf_op jit(solution)/shard_map/while/body/eval_jaxpr/dot_general | solution.py:32
  189.1 2.0 copy.14
  191.1 2.7 %reshape.129 = f32[17,128,2,128]{3,2,1,0:T(2,128)S(1)} reshape(f32[2176,256]{1,0:T(8,128)} %copy.14) | data formatting | bytes 4456448 | tf_op jit(solution)/shard_map/while/body/eval_jaxpr/reshape | solution.py:35
  194.9 3.9 %convolution_bitcast_fusion.3 = f32[2176,256]{0,1:T(8,128)S(1)} fusion(bf16[2176,1024]{1,0:T(8,128)(2,1)} %get-tuple-element.244, bf16[2176,1024]{1,0:T(8,128)(2,1)} %get-tuple-element.243, s32[]{:T(128)S(6)} %select_n.83), kind=kOutput, calls=%fused_computation.1.clone.1 | convolution fusion | flops 1140850688 | bytes 7208964 | tf_op jit(solution)/shard_map/while/body/eval_jaxpr/dot_general | solution.py:32
  198.8 2.0 copy.14
  200.7 2.7 %reshape.129 = f32[17,128,2,128]{3,2,1,0:T(2,128)S(1)} reshape(f32[2176,256]{1,0:T(8,128)} %copy.14) | data formatting | bytes 4456448 | tf_op jit(solution)/shard_map/while/body/eval_jaxpr/reshape | solution.py:35
  (91 shorter events, 22.2 us)
Async XLA Ops:
  6.5 66.1 %all-gather.2.cloned.1.call-start = ((), (), s32[]{:S(2)}) async-start(), calls=%async_computation | async-start | bytes 4456448 | tf_op jit(solution)/shard_map/all_gather | solution.py:54
  14.2 5.1 %copy-start.1 = (s32[17]{0:T(128)S(1)}, s32[17]{0:T(128)}, u32[]{:S(2)}) copy-start(s32[17]{0:T(128)} %param.7) | copy-start | bytes 208
  14.2 5.2 %copy-start = (s32[2048]{0:T(1024)S(1)}, s32[2048]{0:T(1024)}, u32[]{:S(2)}) copy-start(s32[2048]{0:T(1024)} %param.6) | copy-start | bytes 24580
Sparse Core Ops, SparseCore 0:
  19.4 53.2 all-gather.1
where the time goes:
time: 213 us; the launch traced here: 212 us
  local copies, waits for them, and re-layouts  97.1 us (46%)
  waiting for transfers between devices  53.3 us (25%)
  matrix products  34.6 us (16%)
  between operations  13.6 us (6%)
  other arithmetic  13 us (6%)
    all_gather x1, waiting for transfers between devices, per_device(): every = lax.all_gather(unit, ('row', 'col'), axis=0, tiled=True)  53.3 us
    gather x51, local copies, waits for them, and re-layouts  35.5 us
    dot_general x8, matrix products, strip_scores(): lax.dot_general(stacked, panel, (((1,), (1,)), ((), ())), preferred_eleme...  30.8 us
    reshape x8, local copies, waits for them, and re-layouts, strip_scores(): scores = scores.reshape(-1, block_rows, width_blocks, block_rows)  22 us
    dot_general x8, local copies, waits for them, and re-layouts, strip_scores(): lax.dot_general(stacked, panel, (((1,), (1,)), ((), ())), preferred_eleme...  15.8 us
    gather x1, local copies, waits for them, and re-layouts, per_device(): ordered = jnp.take(every, block_order, axis=0)  13.7 us
    reshape x1, local copies, waits for them, and re-layouts, per_device(): windows = spectra.reshape(block_rows * coarse_len // group, TAPS * group)  7.39 us
    reduce_max x8, other arithmetic, strip_scores(): return jnp.max(scores, axis=0)  6.83 us
  transfers between devices with their start and end apart: 1, of which 1 were waited for; matrix products, arithmetic and copies ran while one was open for 0% of the time, Pallas kernels for 0%

commit v1 on v0

v1 whole, which is shorter than its diff:
```python
import functools
import math

import jax
import jax.numpy as jnp
import ml_dtypes
import numpy as np
from jax import lax
from jax.experimental import pallas as pl
from jax.experimental.pallas import tpu as pltpu
from jax.sharding import PartitionSpec as P

TAPS = 16
LANE = 128
WIN = 256
MESH = pl.DeviceIdType.MESH
UP, DOWN, ACROSS, SIB = range(4)


def decimation_weights():
    steps = np.arange(TAPS, dtype=np.float64)
    taps = (0.5 - 0.5 * np.cos(2.0 * math.pi * (steps + 0.5) / TAPS)).astype(ml_dtypes.bfloat16)
    full = np.kron(np.eye(LANE), taps.astype(np.float64)[:, None])
    return full.astype(ml_dtypes.bfloat16)


def kernel(cfg, off_ref, spec_ref, w_ref, bo_ref, out_ref,
           raw, coarse, buf, mine, stack, acc, perm, pick, hilo,
           in_sem, send_sem, recv_sem):
    nz, ny, nb, rows, feats, offs, keep_perm = cfg
    chunks = [(0, 3)] + [(t, min(2, feats // LANE - t)) for t in range(3, feats // LANE, 2)]
    nk = len(chunks)
    total = nb * rows
    tiles = total // WIN
    bins_part = TAPS * LANE

    row = lax.axis_index("row")
    core = lax.axis_index("col")
    z = row // ny
    y = row % ny
    me = row * 2 + core

    def block(zz, yy, cc):
        return (zz * ny + yy) * 2 + cc

    def target(way):
        if way == UP:
            return {"row": row + ny, "col": core}
        if way == DOWN:
            return {"row": row - ny, "col": core}
        if way == ACROSS:
            return {"row": z * ny + (1 - y), "col": core}
        return {"row": row, "col": 1 - core}

    def copy_of(k, blk, way):
        first, count = chunks[k]
        ref = buf.at[pl.ds(first, count), blk]
        return pltpu.make_async_remote_copy(
            src_ref=ref, dst_ref=ref,
            send_sem=send_sem.at[k, way, blk], recv_sem=recv_sem.at[k, blk],
            device_id=target(way), device_id_type=MESH)

    def arrived(k, blk):
        copy_of(k, blk, SIB).wait_recv()

    has_up = z < nz - 1
    has_down = z > 0

    loads = []
    for g in range(feats // LANE):
        load = pltpu.make_async_copy(
            spec_ref.at[:, pl.ds(g * bins_part, bins_part)], raw.at[g], in_sem.at[g])
        load.start()
        loads.append(load)

    barrier = pltpu.get_barrier_semaphore()

    def greet(way):
        pl.semaphore_signal(barrier, inc=1, device_id=target(way), device_id_type=MESH)

    greet(SIB)
    if ny == 2:
        greet(ACROSS)
    pl.when(has_up)(lambda: greet(UP))
    pl.when(has_down)(lambda: greet(DOWN))

    square = jnp.zeros((rows, 1), jnp.float32)
    pair = 2
    for g in range(0, feats // LANE, pair):
        for h in range(pair):
            loads[g + h].wait()
        x = jnp.concatenate([raw[g + h] for h in range(pair)], axis=0)
        c = jnp.dot(x, w_ref[...], preferred_element_type=jnp.float32)
        for h in range(pair):
            part = c[h * rows:(h + 1) * rows]
            coarse[g + h] = part
            square += jnp.sum(part * part, axis=1, keepdims=True)
    scale = lax.rsqrt(square * (1.0 / feats) + 1e-06) * (1.0 / math.sqrt(feats))
    for g in range(feats // LANE):
        buf[g, me] = (coarse[g] * scale).astype(jnp.bfloat16)

    pl.semaphore_wait(barrier, 1 + (1 if ny == 2 else 0)
                      + jnp.where(has_up, 1, 0) + jnp.where(has_down, 1, 0))

    def send_own(k):
        pl.when(has_up)(lambda: copy_of(k, me, UP).start())
        pl.when(has_down)(lambda: copy_of(k, me, DOWN).start())
        if ny == 2:
            copy_of(k, me, ACROSS).start()
        copy_of(k, me, SIB).start()

    def phase(k, t):
        if t < nz:
            @pl.when(z >= t)
            def _():
                blk = block(z - t, y, core)
                arrived(k, blk)
                pl.when(has_up)(lambda: copy_of(k, blk, UP).start())
                if ny == 2:
                    copy_of(k, blk, ACROSS).start()
                copy_of(k, blk, SIB).start()

            @pl.when(z + t < nz)
            def _():
                blk = block(z + t, y, core)
                arrived(k, blk)
                pl.when(has_down)(lambda: copy_of(k, blk, DOWN).start())
                if ny == 2:
                    copy_of(k, blk, ACROSS).start()
                copy_of(k, blk, SIB).start()
        if ny == 2:
            d = t - 1

            def across(blk):
                arrived(k, blk)
                copy_of(k, blk, SIB).start()

            pl.when(z >= d)(lambda: across(block(z - d, 1 - y, core)))
            if d > 0:
                pl.when(z + d < nz)(lambda: across(block(z + d, 1 - y, core)))

    def finish(k):
        for r in range(nb // 2):
            arrived(k, r * 2 + (1 - core))

    send_own(0)

    mine_pos = jnp.transpose(
        jnp.broadcast_to(bo_ref[pl.ds(me, 1), :].astype(jnp.float32), (LANE, LANE)))
    lane_ids = lax.broadcasted_iota(jnp.int32, (rows, LANE), 1).astype(jnp.float32)
    for b in range(nb):
        pick[:, b * LANE:(b + 1) * LANE] = jnp.where(
            mine_pos == lane_ids + float(b * LANE), 1.0, 0.0).astype(jnp.bfloat16)
    mine[:, :LANE] = jnp.zeros((rows, LANE), jnp.float32)
    mine[:, LANE + feats:] = jnp.zeros((rows, LANE), jnp.float32)

    def perm_tile(q):
        ids = lax.broadcasted_iota(jnp.int32, (total, LANE), 0)
        return jnp.where(ids == bo_ref[pl.ds(q, 1), :], 1.0, 0.0).astype(jnp.bfloat16)

    def build(q):
        perm[q] = perm_tile(q)

    for t in range(1, nz + 1):
        if keep_perm:
            per = -(-nb // nz)

            def fill(q, carry):
                build(q)
                return carry

            lax.fori_loop(min((t - 1) * per, nb), min(t * per, nb), fill, 0)
        if t == max(nz - 1, 1) and nk > 1:
            send_own(1)
        phase(0, t)
    finish(0)

    def window(k):
        first, count = chunks[k]
        got = jnp.concatenate(
            [buf[first + i].reshape(total, LANE) for i in range(count)], axis=1)
        mine[:, LANE * (1 + first):LANE * (1 + first + count)] = jnp.dot(
            pick[...], got, preferred_element_type=jnp.float32)
        span = mine[:, WIN * k:WIN * (k + 2)]
        for d in range(offs):
            shift = off_ref[d]
            shift = jnp.where(shift < 0, shift + 2 * WIN, shift)
            moved = pltpu.roll(span, shift, 1)
            stack[d * rows:(d + 1) * rows, :] = moved[:, LANE:LANE + WIN].astype(jnp.bfloat16)

        last = k == nk - 1

        def tile(i, carry):
            right = jnp.concatenate(
                [buf[2 * k + h, pl.ds(2 * i, 2)].reshape(WIN, LANE) for h in range(2)], axis=1)
            s = lax.dot_general(stack[...], right, (((1,), (1,)), ((), ())),
                                preferred_element_type=jnp.float32)
            if k == 0:
                acc[i] = s
            elif not last:
                acc[i] = acc[i] + s
            else:
                best = None
                for d in range(offs):
                    v = acc[i, d * rows:(d + 1) * rows] + s[d * rows:(d + 1) * rows]
                    best = v if best is None else jnp.maximum(best, v)
                high = best.astype(jnp.bfloat16)
                low = (best - high.astype(jnp.float32)).astype(jnp.bfloat16)
                hilo[i] = jnp.concatenate([high, low], axis=0)
            if not last:
                for t in range(1, nz + 1):
                    @pl.when(i == (t - 1) * tiles // nz)
                    def _():
                        if t == max(nz - 1, 1) and k + 2 < nk:
                            send_own(k + 2)
                        phase(k + 1, t)
            return carry

        lax.fori_loop(0, tiles, tile, 0)
        if not last:
            finish(k + 1)

    for k in range(nk):
        window(k)

    def order(q, carry):
        if keep_perm:
            right = jnp.concatenate([perm[2 * q], perm[2 * q + 1]], axis=1)
        else:
            right = jnp.concatenate([perm_tile(2 * q), perm_tile(2 * q + 1)], axis=1)
        left = jnp.concatenate([hilo[i] for i in range(tiles)], axis=1)
        o = jnp.dot(left, right, preferred_element_type=jnp.float32)
        out_ref[:, pl.ds(pl.multiple_of(q * WIN, WIN), WIN)] = o[:rows] + o[rows:]
        return carry

    lax.fori_loop(0, tiles, order, 0)

    for k in range(nk):
        for d in range(nz):
            below = block(z - d, y, core)
            above = block(z + d, y, core)

            @pl.when(z >= d)
            def _():
                pl.when(has_up)(lambda: copy_of(k, below, UP).wait_send())
                if ny == 2:
                    copy_of(k, below, ACROSS).wait_send()

            @pl.when(z + d < nz)
            def _():
                pl.when(has_down)(lambda: copy_of(k, above, DOWN).wait_send())
                if ny == 2 and d > 0:
                    copy_of(k, above, ACROSS).wait_send()
        for r in range(nb // 2):
            copy_of(k, r * 2 + core, SIB).wait_send()


def per_device(spectra, block_order, offsets):
    rows, bins = spectra.shape
    feats = bins // TAPS
    offs = offsets.shape[0]
    nrow, ncol = lax.axis_size("row"), lax.axis_size("col")
    nb = nrow * ncol
    total = nb * rows
    ny = 2 if nrow % 2 == 0 else 1
    nz = nrow // ny
    nk = (feats // LANE - 3 + 1) // 2 + 1
    keep_perm = total <= 2048
    cfg = (nz, ny, nb, rows, feats, offs, keep_perm)
    bf, f32 = jnp.bfloat16, jnp.float32
    any_space = pl.BlockSpec(memory_space=pl.ANY)
    vmem = pl.BlockSpec(memory_space=pltpu.VMEM)
    return pl.pallas_call(
        functools.partial(kernel, cfg),
        out_shape=jax.ShapeDtypeStruct((rows, total), f32),
        in_specs=[pl.BlockSpec(memory_space=pltpu.SMEM), any_space, vmem, vmem],
        out_specs=vmem,
        scratch_shapes=[
            pltpu.VMEM((feats // LANE, rows, TAPS * LANE), bf),
            pltpu.VMEM((feats // LANE, rows, LANE), f32),
            pltpu.VMEM((feats // LANE, nb, rows, LANE), bf),
            pltpu.VMEM((rows, feats + 2 * LANE), f32),
            pltpu.VMEM((offs * rows, WIN), bf),
            pltpu.VMEM((total // WIN, offs * rows, WIN), f32),
            pltpu.VMEM((nb, total, LANE) if keep_perm else (1, 16, LANE), bf),
            pltpu.VMEM((rows, total), bf),
            pltpu.VMEM((total // WIN, 2 * rows, WIN), bf),
            pltpu.SemaphoreType.DMA((feats // LANE,)),
            pltpu.SemaphoreType.DMA((nk, 4, nb)),
            pltpu.SemaphoreType.DMA((nk, nb)),
        ],
        compiler_params=pltpu.CompilerParams(
            collective_id=0, has_side_effects=True, vmem_limit_bytes=60 * 1024 * 1024),
    )(offsets, spectra, jnp.asarray(decimation_weights()), block_order.reshape(nb, rows))


def solution(mesh):
    in_specs = (P(("groups", "row", "col"), None), P("groups"), P())
    out_specs = P(("groups", "row", "col"), None)
    return jax.shard_map(
        per_device, mesh=mesh, in_specs=in_specs, out_specs=out_specs, check_vma=False
    )
```

time: 213 us -> 70 us (0.33)
  local copies, waits for them, and re-layouts: 97.1 us -> 2.3 us
  Pallas kernels: 0 us -> 67.3 us
  waiting for transfers between devices: 53.3 us -> 0 us
  matrix products: 34.6 us -> 0 us
  between operations: 13.6 us -> 0.01 us
  other arithmetic: 13 us -> 0 us
    pallas_call x0 -> x1, Pallas kernels: none -> 67.3 us  [per_device(): pl.pallas_call(functools.partial(kernel, cfg), out_shape=jax.ShapeDtypeSt...]
    all_gather x1 -> x0, waiting for transfers between devices: 53.3 us -> none  [per_device(): every = lax.all_gather(unit, ('row', 'col'), axis=0, tiled=True)]
    gather x52 -> x0, local copies, waits for them, and re-layouts: 49.3 us -> none
    dot_general x9 -> x0, matrix products: 34.6 us -> none  [the longest x8 30.8 us: strip_scores(): lax.dot_general(stacked, panel, (((1,), (1,)), ((), ())), preferred_eleme...]
    reshape x11 -> x0, local copies, waits for them, and re-layouts: 30.5 us -> none  [the longest x8 22 us: strip_scores(): scores = scores.reshape(-1, block_rows, width_blocks, block_rows)]
    dot_general x9 -> x0, local copies, waits for them, and re-layouts: 15.9 us -> none  [the longest x8 15.8 us: strip_scores(): lax.dot_general(stacked, panel, (((1,), (1,)), ((), ())), preferred_eleme...]
    reduce_max x8 -> x0, other arithmetic: 6.83 us -> none  [strip_scores(): return jnp.max(scores, axis=0)]
    concatenate x1 -> x0, other arithmetic: 2.52 us -> none  [per_device(): extended = jnp.concatenate([ordered, ordered[:block_rows]], axis=0)]
  transfers between devices with their start and end apart: 1 -> 0, of which waited for: 1 -> 0; matrix products, arithmetic and copies ran while one was open for 0% -> 0% of each run, Pallas kernels for 0% -> 0%
where the time goes in v1:
time: 70 us; the launch traced here: 69.6 us
  Pallas kernels  67.3 us (96%)
  local copies, waits for them, and re-layouts  2.3 us (3%)
    pallas_call x1, Pallas kernels, per_device(): pl.pallas_call(functools.partial(kernel, cfg), out_shape=jax.ShapeDtypeSt...  67.3 us
    unnamed x1, local copies, waits for them, and re-layouts  2.3 us

profile of v1, /device:TPU:0, one launch (start us, length us, event | category | flops | bytes accessed | tf_op | source)
XLA Modules:
  0.0 69.6 jit_solution(7172485968013382826)
XLA Ops:
  0.0 67.3 %shard_map.46 = f32[128,2048]{1,0:T(8,128)} custom-call(s32[17]{0:T(128)} %off_ref.1, bf16[128,16384]{1,0:T(8,128)(2,1)} %spec_ref.1, bf16[2048,128]{1,0:T(8,128)(2,1)} %constant.2.clone.w_ref, s32[16,128]{1,0:T(8,128)} %bitcast.1), custom_call_target="tpu_custom_call" | custom-call | tf_op jit(solution)/shard_map/pallas_call | solution.py:273
  67.3 2.3 %copy.6 = f32[128,2048]{1,0:T(8,128)} copy(f32[128,2048]{1,0:T(8,128)} %shard_map.46) | data formatting | bytes 2097152

commit v2 on v1

--- a/solution.py
+++ b/solution.py
@@ -13,6 +13,7 @@
 TAPS = 16
 LANE = 128
 WIN = 256
+GROUP = 17
 MESH = pl.DeviceIdType.MESH
 UP, DOWN, ACROSS, SIB = range(4)
 
@@ -25,9 +26,9 @@
 
 
 def kernel(cfg, off_ref, spec_ref, w_ref, bo_ref, out_ref,
-           raw, coarse, buf, mine, stack, acc, perm, pick, hilo,
+           raw, coarse, buf, mine, stack, acc, pick,
            in_sem, send_sem, recv_sem):
-    nz, ny, nb, rows, feats, offs, keep_perm = cfg
+    nz, ny, nb, rows, feats, offs = cfg
     chunks = [(0, 3)] + [(t, min(2, feats // LANE - t)) for t in range(3, feats // LANE, 2)]
     nk = len(chunks)
     total = nb * rows
@@ -109,41 +110,55 @@
             copy_of(k, me, ACROSS).start()
         copy_of(k, me, SIB).start()
 
-    def phase(k, t):
-        if t < nz:
-            @pl.when(z >= t)
-            def _():
-                blk = block(z - t, y, core)
-                arrived(k, blk)
-                pl.when(has_up)(lambda: copy_of(k, blk, UP).start())
-                if ny == 2:
-                    copy_of(k, blk, ACROSS).start()
-                copy_of(k, blk, SIB).start()
-
-            @pl.when(z + t < nz)
-            def _():
-                blk = block(z + t, y, core)
-                arrived(k, blk)
-                pl.when(has_down)(lambda: copy_of(k, blk, DOWN).start())
-                if ny == 2:
-                    copy_of(k, blk, ACROSS).start()
-                copy_of(k, blk, SIB).start()
-        if ny == 2:
-            d = t - 1
-
-            def across(blk):
-                arrived(k, blk)
-                copy_of(k, blk, SIB).start()
-
-            pl.when(z >= d)(lambda: across(block(z - d, 1 - y, core)))
-            if d > 0:
-                pl.when(z + d < nz)(lambda: across(block(z + d, 1 - y, core)))
+    def onward(k, t):
+        @pl.when(z >= t)
+        def _():
+            blk = block(z - t, y, core)
+            arrived(k, blk)
+            pl.when(has_up)(lambda: copy_of(k, blk, UP).start())
+            if ny == 2:
+                copy_of(k, blk, ACROSS).start()
+            copy_of(k, blk, SIB).start()
+
+        @pl.when(z + t < nz)
+        def _():
+            blk = block(z + t, y, core)
+            arrived(k, blk)
+            pl.when(has_down)(lambda: copy_of(k, blk, DOWN).start())
+            if ny == 2:
+                copy_of(k, blk, ACROSS).start()
+            copy_of(k, blk, SIB).start()
+
+    def share(k, d):
+        def across(blk):
+            arrived(k, blk)
+            copy_of(k, blk, SIB).start()
+
+        pl.when(z >= d)(lambda: across(block(z - d, 1 - y, core)))
+        if d > 0:
+            pl.when(z + d < nz)(lambda: across(block(z + d, 1 - y, core)))
 
     def finish(k):
         for r in range(nb // 2):
             arrived(k, r * 2 + (1 - core))
 
-    send_own(0)
+    events = []
+    for k in range(nk):
+        events.append((2 * k - 0.5, functools.partial(send_own, k)))
+        for t in range(1, nz):
+            events.append((2 * k + t, functools.partial(onward, k, t)))
+        for d in range(nz if ny == 2 else 0):
+            events.append((2 * k + d + 1.6, functools.partial(share, k, d)))
+        events.append((2 * k + nz + 1, functools.partial(finish, k)))
+    events.sort(key=lambda e: e[0])
+
+    def due(k):
+        low = 2 * (k - 1) + nz + 1 if k > 0 else -1
+        high = 2 * k + nz + 1
+        return [run for key, run in events if low < key <= high]
+
+    first_due = due(0)
+    first_due[0]()
 
     mine_pos = jnp.transpose(
         jnp.broadcast_to(bo_ref[pl.ds(me, 1), :].astype(jnp.float32), (LANE, LANE)))
@@ -154,26 +169,8 @@
     mine[:, :LANE] = jnp.zeros((rows, LANE), jnp.float32)
     mine[:, LANE + feats:] = jnp.zeros((rows, LANE), jnp.float32)
 
-    def perm_tile(q):
-        ids = lax.broadcasted_iota(jnp.int32, (total, LANE), 0)
-        return jnp.where(ids == bo_ref[pl.ds(q, 1), :], 1.0, 0.0).astype(jnp.bfloat16)
-
-    def build(q):
-        perm[q] = perm_tile(q)
-
-    for t in range(1, nz + 1):
-        if keep_perm:
-            per = -(-nb // nz)
-
-            def fill(q, carry):
-                build(q)
-                return carry
-
-            lax.fori_loop(min((t - 1) * per, nb), min(t * per, nb), fill, 0)
-        if t == max(nz - 1, 1) and nk > 1:
-            send_own(1)
-        phase(0, t)
-    finish(0)
+    for run in first_due[1:]:
+        run()
 
     def window(k):
         first, count = chunks[k]
@@ -189,51 +186,40 @@
             stack[d * rows:(d + 1) * rows, :] = moved[:, LANE:LANE + WIN].astype(jnp.bfloat16)
 
         last = k == nk - 1
+        todo = [] if last else due(k + 1)
 
         def tile(i, carry):
             right = jnp.concatenate(
                 [buf[2 * k + h, pl.ds(2 * i, 2)].reshape(WIN, LANE) for h in range(2)], axis=1)
-            s = lax.dot_general(stack[...], right, (((1,), (1,)), ((), ())),
-                                preferred_element_type=jnp.float32)
-            if k == 0:
-                acc[i] = s
-            elif not last:
-                acc[i] = acc[i] + s
-            else:
-                best = None
-                for d in range(offs):
-                    v = acc[i, d * rows:(d + 1) * rows] + s[d * rows:(d + 1) * rows]
-                    best = v if best is None else jnp.maximum(best, v)
-                high = best.astype(jnp.bfloat16)
-                low = (best - high.astype(jnp.float32)).astype(jnp.bfloat16)
-                hilo[i] = jnp.concatenate([high, low], axis=0)
-            if not last:
-                for t in range(1, nz + 1):
-                    @pl.when(i == (t - 1) * tiles // nz)
+            best = None
+            for d0 in range(0, offs, GROUP):
+                d1 = min(d0 + GROUP, offs)
+                s = lax.dot_general(stack[d0 * rows:d1 * rows, :], right, (((1,), (1,)), ((), ())),
+                                    preferred_element_type=jnp.float32)
+                if k == 0:
+                    acc[i, d0 * rows:d1 * rows, :] = s
+                elif not last:
+                    acc[i, d0 * rows:d1 * rows, :] += s
+                else:
+                    s = acc[i, d0 * rows:d1 * rows, :] + s
+                    for d in range(d1 - d0):
+                        v = s[d * rows:(d + 1) * rows]
+                        best = v if best is None else jnp.maximum(best, v)
+            if last:
+                out_ref[pl.ds(pl.multiple_of(i * WIN, WIN), WIN), :] = jnp.transpose(best)
+            for slot in range(tiles):
+                now = [run for j, run in enumerate(todo) if j * tiles // len(todo) == slot]
+                if now:
+                    @pl.when(i == slot)
                     def _():
-                        if t == max(nz - 1, 1) and k + 2 < nk:
-                            send_own(k + 2)
-                        phase(k + 1, t)
+                        for run in now:
+                            run()
             return carry
 
         lax.fori_loop(0, tiles, tile, 0)
-        if not last:
-            finish(k + 1)
 
     for k in range(nk):
         window(k)
-
-    def order(q, carry):
-        if keep_perm:
-            right = jnp.concatenate([perm[2 * q], perm[2 * q + 1]], axis=1)
-        else:
-            right = jnp.concatenate([perm_tile(2 * q), perm_tile(2 * q + 1)], axis=1)
-        left = jnp.concatenate([hilo[i] for i in range(tiles)], axis=1)
-        o = jnp.dot(left, right, preferred_element_type=jnp.float32)
-        out_ref[:, pl.ds(pl.multiple_of(q * WIN, WIN), WIN)] = o[:rows] + o[rows:]
-        return carry
-
-    lax.fori_loop(0, tiles, order, 0)
 
     for k in range(nk):
         for d in range(nz):
@@ -253,6 +239,21 @@
                     copy_of(k, above, ACROSS).wait_send()
         for r in range(nb // 2):
             copy_of(k, r * 2 + core, SIB).wait_send()
+
+
+def order_kernel(bo_ref, scores_ref, out_ref, gathered):
+    total = scores_ref.shape[0]
+    unroll = 16
+
+    def some(g, carry):
+        base = pl.multiple_of(g * unroll, unroll)
+        for h in range(unroll):
+            gathered[pl.ds(base + h, 1), :] = scores_ref[pl.ds(bo_ref[base + h], 1), :]
+        return carry
+
+    for t in range(total // LANE):
+        lax.fori_loop(t * LANE // unroll, (t + 1) * LANE // unroll, some, 0)
+        out_ref[:, t * LANE:(t + 1) * LANE] = jnp.transpose(gathered[t * LANE:(t + 1) * LANE, :])
 
 
 def per_device(spectra, block_order, offsets):
@@ -265,14 +266,13 @@
     ny = 2 if nrow % 2 == 0 else 1
     nz = nrow // ny
     nk = (feats // LANE - 3 + 1) // 2 + 1
-    keep_perm = total <= 2048
-    cfg = (nz, ny, nb, rows, feats, offs, keep_perm)
+    cfg = (nz, ny, nb, rows, feats, offs)
     bf, f32 = jnp.bfloat16, jnp.float32
     any_space = pl.BlockSpec(memory_space=pl.ANY)
     vmem = pl.BlockSpec(memory_space=pltpu.VMEM)
-    return pl.pallas_call(
+    scores = pl.pallas_call(
         functools.partial(kernel, cfg),
-        out_shape=jax.ShapeDtypeStruct((rows, total), f32),
+        out_shape=jax.ShapeDtypeStruct((total, rows), f32),
         in_specs=[pl.BlockSpec(memory_space=pltpu.SMEM), any_space, vmem, vmem],
         out_specs=vmem,
         scratch_shapes=[
@@ -282,9 +282,7 @@
             pltpu.VMEM((rows, feats + 2 * LANE), f32),
             pltpu.VMEM((offs * rows, WIN), bf),
             pltpu.VMEM((total // WIN, offs * rows, WIN), f32),
-            pltpu.VMEM((nb, total, LANE) if keep_perm else (1, 16, LANE), bf),
             pltpu.VMEM((rows, total), bf),
-            pltpu.VMEM((total // WIN, 2 * rows, WIN), bf),
             pltpu.SemaphoreType.DMA((feats // LANE,)),
             pltpu.SemaphoreType.DMA((nk, 4, nb)),
             pltpu.SemaphoreType.DMA((nk, nb)),
@@ -292,6 +290,14 @@
         compiler_params=pltpu.CompilerParams(
             collective_id=0, has_side_effects=True, vmem_limit_bytes=60 * 1024 * 1024),
     )(offsets, spectra, jnp.asarray(decimation_weights()), block_order.reshape(nb, rows))
+    return pl.pallas_call(
+        order_kernel,
+        out_shape=jax.ShapeDtypeStruct((rows, total), f32),
+        in_specs=[pl.BlockSpec(memory_space=pltpu.SMEM), vmem],
+        out_specs=vmem,
+        scratch_shapes=[pltpu.VMEM((total, rows), f32)],
+        compiler_params=pltpu.CompilerParams(vmem_limit_bytes=16 * 1024 * 1024),
+    )(block_order, scores)
 
 
 def solution(mesh):

time: 70 us -> 59 us (0.84)
  Pallas kernels: 67.3 us -> 57.6 us
  local copies, waits for them, and re-layouts: 2.3 us -> 1.22 us
    pallas_call x1, Pallas kernels: 67.3 us -> 52.2 us  [per_device(): pl.pallas_call(functools.partial(kernel, cfg), out_shape=jax.ShapeDtypeSt...]
    pallas_call x0 -> x1, Pallas kernels: none -> 5.35 us  [per_device(): pl.pallas_call(order_kernel, out_shape=jax.ShapeDtypeStruct((rows, total)...]
    unnamed x1 -> x4, local copies, waits for them, and re-layouts: 2.3 us -> 1.22 us
where the time goes in v2:
time: 59 us; the launch traced here: 58.8 us
  Pallas kernels  57.6 us (98%)
  local copies, waits for them, and re-layouts  1.22 us (2%)
    pallas_call x1, Pallas kernels, per_device(): pl.pallas_call(functools.partial(kernel, cfg), out_shape=jax.ShapeDtypeSt...  52.2 us
    pallas_call x1, Pallas kernels, per_device(): pl.pallas_call(order_kernel, out_shape=jax.ShapeDtypeStruct((rows, total)...  5.35 us
    unnamed x4, local copies, waits for them, and re-layouts  1.22 us

profile of v2, /device:TPU:0, one launch (start us, length us, event | category | flops | bytes accessed | tf_op | source)
XLA Modules:
  0.0 58.8 jit_solution(7377566183846946794)
XLA Ops:
  0.0 0.0 copy-start.1
  0.0 52.2 %shard_map.46.scores_ref = f32[2048,128]{1,0:T(8,128)} custom-call(s32[17]{0:T(128)} %off_ref.1, bf16[128,16384]{1,0:T(8,128)(2,1)} %spec_ref.1, bf16[2048,128]{1,0:T(8,128)(2,1)} %constant.2.clone.w_ref, s32[16,128]{1,0:T(8,128)} %bitcast.1), custom_call_target="tpu_custom_call" | custom-call | tf_op jit(solution)/shard_map/pallas_call | solution.py:273
  52.2 0.0 copy-done.1
  52.2 0.0 copy-start
  52.3 1.2 %copy-done = f32[2048,128]{1,0:T(8,128)S(1)} copy-done((f32[2048,128]{1,0:T(8,128)S(1)}, f32[2048,128]{1,0:T(8,128)}, u32[]{:S(2)}) %copy-start) | copy-done | bytes 1048600
  53.5 5.3 %shard_map.47 = f32[128,2048]{1,0:T(8,128)} custom-call(s32[2048]{0:T(1024)S(1)} %copy-done.1, f32[2048,128]{1,0:T(8,128)S(1)} %copy-done), custom_call_target="tpu_custom_call" | custom-call | tf_op jit(solution)/shard_map/pallas_call | solution.py:293
Async XLA Ops:
  0.0 52.2 %copy-start.1 = (s32[2048]{0:T(1024)S(1)}, s32[2048]{0:T(1024)}, u32[]{:S(2)}) copy-start(s32[2048]{0:T(1024)} %bo_ref.1) | copy-start | bytes 24580
  52.2 1.2 %copy-start = (f32[2048,128]{1,0:T(8,128)S(1)}, f32[2048,128]{1,0:T(8,128)}, u32[]{:S(2)}) copy-start(f32[2048,128]{1,0:T(8,128)} %shard_map.46.scores_ref) | copy-start | bytes 3145732

commit v3 on v2

--- a/solution.py
+++ b/solution.py
@@ -13,7 +13,8 @@
 TAPS = 16
 LANE = 128
 WIN = 256
-GROUP = 17
+GROUP = 2
+TW = 1024
 MESH = pl.DeviceIdType.MESH
 UP, DOWN, ACROSS, SIB = range(4)
 
@@ -32,7 +33,7 @@
     chunks = [(0, 3)] + [(t, min(2, feats // LANE - t)) for t in range(3, feats // LANE, 2)]
     nk = len(chunks)
     total = nb * rows
-    tiles = total // WIN
+    tiles = total // TW
     bins_part = TAPS * LANE
 
     row = lax.axis_index("row")
@@ -149,12 +150,12 @@
             events.append((2 * k + t, functools.partial(onward, k, t)))
         for d in range(nz if ny == 2 else 0):
             events.append((2 * k + d + 1.6, functools.partial(share, k, d)))
-        events.append((2 * k + nz + 1, functools.partial(finish, k)))
+        events.append((2 * k + nz + 1.1, functools.partial(finish, k)))
     events.sort(key=lambda e: e[0])
 
     def due(k):
-        low = 2 * (k - 1) + nz + 1 if k > 0 else -1
-        high = 2 * k + nz + 1
+        low = 2 * (k - 1) + nz + 1.1 if k > 0 else -10
+        high = 2 * k + nz + 1.1
         return [run for key, run in events if low < key <= high]
 
     first_due = due(0)
@@ -190,7 +191,7 @@
 
         def tile(i, carry):
             right = jnp.concatenate(
-                [buf[2 * k + h, pl.ds(2 * i, 2)].reshape(WIN, LANE) for h in range(2)], axis=1)
+                [buf[2 * k + h, pl.ds(TW // LANE * i, TW // LANE)].reshape(TW, LANE) for h in range(2)], axis=1)
             best = None
             for d0 in range(0, offs, GROUP):
                 d1 = min(d0 + GROUP, offs)
@@ -206,7 +207,7 @@
                         v = s[d * rows:(d + 1) * rows]
                         best = v if best is None else jnp.maximum(best, v)
             if last:
-                out_ref[pl.ds(pl.multiple_of(i * WIN, WIN), WIN), :] = jnp.transpose(best)
+                out_ref[pl.ds(pl.multiple_of(i * TW, TW), TW), :] = jnp.transpose(best)
             for slot in range(tiles):
                 now = [run for j, run in enumerate(todo) if j * tiles // len(todo) == slot]
                 if now:
@@ -281,7 +282,7 @@
             pltpu.VMEM((feats // LANE, nb, rows, LANE), bf),
             pltpu.VMEM((rows, feats + 2 * LANE), f32),
             pltpu.VMEM((offs * rows, WIN), bf),
-            pltpu.VMEM((total // WIN, offs * rows, WIN), f32),
+            pltpu.VMEM((total // TW, offs * rows, TW), f32),
             pltpu.VMEM((rows, total), bf),
             pltpu.SemaphoreType.DMA((feats // LANE,)),
             pltpu.SemaphoreType.DMA((nk, 4, nb)),

time: 59 us -> 55.7 us (0.944)
  Pallas kernels: 57.6 us -> 54.3 us
    pallas_call x1, Pallas kernels: 52.2 us -> 49 us  [per_device(): pl.pallas_call(functools.partial(kernel, cfg), out_shape=jax.ShapeDtypeSt...]
where the time goes in v3:
time: 55.7 us; the launch traced here: 55.6 us
  Pallas kernels  54.3 us (97%)
  local copies, waits for them, and re-layouts  1.22 us (2%)
    pallas_call x1, Pallas kernels, per_device(): pl.pallas_call(functools.partial(kernel, cfg), out_shape=jax.ShapeDtypeSt...  49 us
    pallas_call x1, Pallas kernels, per_device(): pl.pallas_call(order_kernel, out_shape=jax.ShapeDtypeStruct((rows, total)...  5.35 us
    unnamed x4, local copies, waits for them, and re-layouts  1.22 us

profile of v3, /device:TPU:0, one launch (start us, length us, event | category | flops | bytes accessed | tf_op | source)
XLA Modules:
  0.0 55.6 jit_solution(10729092785898882383)
XLA Ops:
  0.0 0.0 copy-start.1
  0.0 49.0 %shard_map.46.scores_ref = f32[2048,128]{1,0:T(8,128)} custom-call(s32[17]{0:T(128)} %off_ref.1, bf16[128,16384]{1,0:T(8,128)(2,1)} %spec_ref.1, bf16[2048,128]{1,0:T(8,128)(2,1)} %constant.2.clone.w_ref, s32[16,128]{1,0:T(8,128)} %bitcast.1), custom_call_target="tpu_custom_call" | custom-call | tf_op jit(solution)/shard_map/pallas_call | solution.py:274
  49.0 0.0 copy-done.1
  49.0 0.0 copy-start
  49.0 1.2 %copy-done = f32[2048,128]{1,0:T(8,128)S(1)} copy-done((f32[2048,128]{1,0:T(8,128)S(1)}, f32[2048,128]{1,0:T(8,128)}, u32[]{:S(2)}) %copy-start) | copy-done | bytes 1048600
  50.2 5.3 %shard_map.47 = f32[128,2048]{1,0:T(8,128)} custom-call(s32[2048]{0:T(1024)S(1)} %copy-done.1, f32[2048,128]{1,0:T(8,128)S(1)} %copy-done), custom_call_target="tpu_custom_call" | custom-call | tf_op jit(solution)/shard_map/pallas_call | solution.py:294
Async XLA Ops:
  0.0 49.0 %copy-start.1 = (s32[2048]{0:T(1024)S(1)}, s32[2048]{0:T(1024)}, u32[]{:S(2)}) copy-start(s32[2048]{0:T(1024)} %bo_ref.1) | copy-start | bytes 24580
  49.0 1.2 %copy-start = (f32[2048,128]{1,0:T(8,128)S(1)}, f32[2048,128]{1,0:T(8,128)}, u32[]{:S(2)}) copy-start(f32[2048,128]{1,0:T(8,128)} %shard_map.46.scores_ref) | copy-start | bytes 3145732
